TPU v7x, 256 devices: a whole 4x4x8 slice. The times are simulated.
256 devices in a mesh: ctx: 8 (over x, y_lo), chan: 32 (over y_hi, z, core).
Axes of the slice: x: 4, y: 4 (y_hi: 2, y_lo: 2; y = y_hi * 2 + y_lo), z: 8, core: 2. Of those that a mesh axis runs over, the one named last changes fastest.
Arguments:
- tokens: bfloat16 [4096, 8192], P('ctx', 'chan'), may hold values from -6 to 6
- in_base: bfloat16 [8192, 3, 4096], P('ctx', None, 'chan'), may hold values from -0.0625 to 0.0625
- in_task: bfloat16 [8192, 3, 4096], P('ctx', None, 'chan'), may hold values from -0.03125 to 0.03125
- feat_weight: float32 [7, 3, 4096], P(None, None, 'chan'), may hold values from -2 to 2
- filter_taps: float32 [128, 4096], P(None, 'chan'), may hold values from -0.5 to 0.5
- decay_rates: float32 [4096], P('chan'), may hold values from 0.002 to 0.08
- skip_gain: float32 [4096], P('chan'), may hold values from -1 to 1
- out_base: bfloat16 [4096, 8192], P('chan', 'ctx'), may hold values from -0.1875 to 0.1875
- out_task: bfloat16 [4096, 8192], P('chan', 'ctx'), may hold values from -0.046875 to 0.046875
Outputs:
- layer_out: bfloat16 [4096, 8192], P('ctx', 'chan')
All inputs are finite; a program needn't handle non-finite values.
Results may differ from a plain program's by a relative error of at most 0.0092.
Values may be sent and summed in bfloat16 or wider, within the bound.
A program may use at most 128 MiB of HBM per device.

v0:
```python
import jax
import jax.numpy as jnp
from jax import lax
from jax.sharding import PartitionSpec as P


def shifted(value, axis, by):
    size = lax.axis_size(axis)
    pairs = [(i, i + by) for i in range(size) if 0 <= i + by < size]
    return lax.ppermute(value, axis, pairs)


def featurize_valid(extended, feat_weight, count):
    taps_short = feat_weight.shape[0]
    result = jnp.zeros((count,) + extended.shape[1:], jnp.float32)
    for offset in range(taps_short):
        begin_at = taps_short - 1 - offset
        result = result + feat_weight[offset] * extended[begin_at : begin_at + count].astype(
            jnp.float32
        )
    return result


def negate_task(base_part, task_part):
    return (base_part.astype(jnp.float32) - task_part.astype(jnp.float32)).astype(jnp.bfloat16)


def shards(
    tokens, in_base, in_task, feat_weight, filter_taps, decay_rates, skip_gain, out_base, out_task
):
    base_all, task_all = (
        lax.all_gather(in_base, "ctx", axis=0, tiled=True),
        lax.all_gather(in_task, "ctx", axis=0, tiled=True),
    )
    in_weight = negate_task(base_all, task_all)
    width_all = in_weight.shape[0]
    chan_local = in_weight.shape[2]
    flat_weight = in_weight.reshape(width_all, 3 * chan_local)
    tok_rows = tokens.shape[0]
    projected = jnp.dot(
        lax.all_gather(tokens, "chan", axis=1, tiled=True),
        flat_weight,
        preferred_element_type=jnp.float32,
    )
    projected = projected.astype(jnp.bfloat16).reshape(tok_rows, 3, chan_local)
    taps_long = filter_taps.shape[0]
    taps_short = feat_weight.shape[0]
    lag_values = jnp.arange(taps_long, dtype=jnp.float32)
    filter_full = filter_taps * jnp.exp(-decay_rates[None, :] * lag_values[:, None])
    rim_rows = shifted(projected[tok_rows - (taps_short - 1) :], "ctx", 1)
    extended = jnp.concatenate([rim_rows, projected], axis=0)
    featured = featurize_valid(extended, feat_weight, tok_rows)
    query_part = featured[:, 0, :]
    own_input = featured[:, 1, :] * featured[:, 2, :]
    input_rim = shifted(own_input[tok_rows - (taps_long - 1) :], "ctx", 1)
    long_input = jnp.concatenate([input_rim, own_input], axis=0)
    mixed = skip_gain * own_input
    conv_sum = jnp.zeros((tok_rows, chan_local), jnp.float32)
    for lag_index in range(taps_long):
        begin_at = taps_long - 1 - lag_index
        conv_sum = conv_sum + filter_full[lag_index] * long_input[begin_at : begin_at + tok_rows]
    mixed = mixed + conv_sum
    gated_out = (query_part * mixed).astype(jnp.bfloat16)
    base_cols, task_cols = (
        lax.all_gather(out_base, "ctx", axis=1, tiled=True),
        lax.all_gather(out_task, "ctx", axis=1, tiled=True),
    )
    out_weight = negate_task(base_cols, task_cols)
    partial_terms = jnp.dot(gated_out, out_weight, preferred_element_type=jnp.float32)
    summed = lax.psum_scatter(partial_terms, "chan", scatter_dimension=1, tiled=True)
    return summed.astype(jnp.bfloat16)


def solution(mesh):
    in_specs = (
        P("ctx", "chan"),
        P("ctx", None, "chan"),
        P("ctx", None, "chan"),
        P(None, None, "chan"),
        P(None, "chan"),
        P("chan"),
        P("chan"),
        P("chan", "ctx"),
        P("chan", "ctx"),
    )
    out_specs = P("ctx", "chan")
    return jax.shard_map(shards, mesh=mesh, in_specs=in_specs, out_specs=out_specs, check_vma=False)
```

profile of v0, /device:TPU:4, one launch (start us, length us, event | category | flops | bytes accessed | tf_op | source)
XLA Modules:
  0.0 755.3 jit_solution(2563523671187403728)
XLA Ops:
  6.5 2.3 copy.10
  8.9 2.3 copy.11
  11.3 0.7 all-gather.10.cloned.1.call-update
  12.0 0.5 all-gather.12.cloned.1.call-update
  12.6 0.5 all-gather.14.cloned.1.call-update
  13.2 0.7 neg.4
  13.9 0.9 exponential_multiply_fusion
  14.9 1.0 fusion.391
  15.9 127.7 %all-gather.6.cloned.1.call-done = bf16[8192,3,128]{0,2,1:T(8,128)(2,1)} async-done(((bf16[1024,3,128]{0,2,1:T(8,128)(2,1)}), bf16[8192,3,128]{0,2,1:T(8,128)(2,1)}) %all-gather.6.cloned.1.call-update) | async-done | bytes 6291472 | tf_op jit(solution)/shard_map/all_gather | solution.py:32
  143.6 134.7 %all-gather.8.cloned.1.call-done = bf16[8192,3,128]{0,2,1:T(8,128)(2,1)} async-done(((bf16[1024,3,128]{0,2,1:T(8,128)(2,1)}), bf16[8192,3,128]{0,2,1:T(8,128)(2,1)}) %all-gather.8.cloned.1.call-update) | async-done | bytes 6291472 | tf_op jit(solution)/shard_map/all_gather | solution.py:33
  278.4 9.9 %subtract_convert_fusion = bf16[8192,3,128]{0,2,1:T(8,128)(2,1)} fusion(bf16[8192,3,128]{0,2,1:T(8,128)(2,1)} %all-gather.8.cloned.1.call-done, bf16[8192,3,128]{0,2,1:T(8,128)(2,1)} %all-gather.6.cloned.1.call-done), kind=kLoop, calls=%fused_computation.126 | loop fusion | flops 12582912 | bytes 18874368 | tf_op jit(solution)/shard_map/convert_element_type | solution.py:25
  288.3 102.3 %all-gather.10.cloned.1.call-done = bf16[512,8192]{1,0:T(8,128)(2,1)} async-done(((bf16[512,256]{1,0:T(8,128)(2,1)}), bf16[512,8192]{1,0:T(8,128)(2,1)}) %all-gather.10.cloned.1.call-update) | async-done | bytes 8388624 | tf_op jit(solution)/shard_map/all_gather | solution.py:41
  390.5 8.6 %convolution_convert_fusion = bf16[384,512]{1,0:T(8,128)(2,1)S(1)} fusion(bf16[8192,384]{0,1:T(8,128)(2,1)} %bitcast.287, bf16[512,8192]{1,0:T(8,128)(2,1)} %all-gather.10.cloned.1.call-done), kind=kOutput, calls=%fused_computation.255 | convolution fusion | flops 3221422080 | bytes 15073280 | tf_op jit(solution)/shard_map/dot_general | solution.py:40
  399.2 0.1 slice.1100
  399.3 2.5 collective-permute-start
  401.8 6.1 collective-permute-done
  407.9 1.5 multiply_add_fusion
  409.4 0.1 slice_bitcast_fusion.1
  409.5 4.6 collective-permute-start.1
  414.1 32.5 %all-gather.12.cloned.1.call-done = bf16[128,8192]{1,0:T(8,128)(2,1)} async-done(((bf16[128,1024]{1,0:T(8,128)(2,1)}), bf16[128,8192]{1,0:T(8,128)(2,1)}) %all-gather.12.cloned.1.call-update) | async-done | bytes 2097168 | tf_op jit(solution)/shard_map/all_gather | solution.py:65
  446.6 55.2 %all-gather.14.cloned.1.call-done = bf16[128,8192]{1,0:T(8,128)(2,1)} async-done(((bf16[128,1024]{1,0:T(8,128)(2,1)}), bf16[128,8192]{1,0:T(8,128)(2,1)}) %all-gather.14.cloned.1.call-update) | async-done | bytes 2097168 | tf_op jit(solution)/shard_map/all_gather | solution.py:66
  501.8 23.9 %fusion = f32[512,8192]{1,0:T(8,128)} fusion(bf16[128,8192]{1,0:T(8,128)(2,1)} %all-gather.14.cloned.1.call-done, bf16[128,8192]{1,0:T(8,128)(2,1)} %all-gather.12.cloned.1.call-done, f32[512,128]{0,1:T(8,128)S(1)} %fusion.394, f32[127,128]{0,1:T(8,128)S(1)} %collective-permute-done.1, f32[512,3,128]{0,2,1:T(8,128)S(1)} %multiply_add_fusion, ...), kind=kOutput, calls=%fused_computation.128 | convolution fusion | flops 1103233024 | bytes 21627392 | tf_op jit(solution)/shard_map/dot_general | solution.py:69
  525.7 221.0 %reduce-scatter.2.cloned.1.call-done = f32[512,256]{1,0:T(8,128)} async-done(((f32[512,8192]{1,0:T(8,128)}), f32[512,256]{1,0:T(8,128)}) %reduce-scatter.2.cloned.1.call-update) | async-done | bytes 524304 | tf_op jit(solution)/shard_map/reduce_scatter | solution.py:70
  746.7 1.8 convert_element_type.67
  (25 shorter events, 0.4 us)
Async XLA Ops:
  6.5 137.1 %all-gather.6.cloned.1.call-start = ((), (), s32[]{:S(2)}) async-start(), calls=%async_computation.1 | async-start | bytes 7077888 | tf_op jit(solution)/shard_map/all_gather | solution.py:32
  8.9 269.5 %all-gather.8.cloned.1.call-start = ((), (), s32[]{:S(2)}) async-start(), calls=%async_computation.2 | async-start | bytes 7077888 | tf_op jit(solution)/shard_map/all_gather | solution.py:33
  11.3 379.3 %all-gather.10.cloned.1.call-start = ((), (), s32[]{:S(2)}) async-start(), calls=%async_computation.3 | async-start | bytes 8650752 | tf_op jit(solution)/shard_map/all_gather | solution.py:41
  12.0 434.6 %all-gather.12.cloned.1.call-start = ((), (), s32[]{:S(2)}) async-start(), calls=%async_computation.4 | async-start | bytes 2359296 | tf_op jit(solution)/shard_map/all_gather | solution.py:65
  12.6 489.2 %all-gather.14.cloned.1.call-start = ((), (), s32[]{:S(2)}) async-start(), calls=%async_computation.5 | async-start | bytes 2359296 | tf_op jit(solution)/shard_map/all_gather | solution.py:66
  13.2 733.5 %reduce-scatter.2.cloned.1.call-start = ((), (), s32[]{:S(2)}) async-start(), calls=%async_computation.6 | async-start | bytes 17301504 | tf_op jit(solution)/shard_map/reduce_scatter | solution.py:70
  390.5 111.3 %copy-start = (f32[128]{0:T(128)S(1)}, f32[128]{0:T(128)}, u32[]{:S(2)}) copy-start(f32[128]{0:T(128)} %param.15) | copy-start | bytes 1540
  399.3 8.6 %collective-permute-start = (bf16[6,3,128]{0,2,1:T(8,128)(2,1)S(1)}, bf16[6,3,128]{0,2,1:T(8,128)(2,1)S(1)}, u32[]{:S(2)}, u32[]{:S(2)}) collective-permute-start(bf16[6,3,128]{0,2,1:T(8,128)(2,1)S(1)} %bitcast.290), channel_id=1, source_target_pairs={{0,32},{32,64},{64,96},{96,128},{128,160},{160,192},{192,224},{1,3... | collective-permute-start | bytes 13832 | tf_op jit(solution)/shard_map/ppermute | solution.py:10
  409.5 92.3 %collective-permute-start.1 = (f32[127,128]{0,1:T(8,128)S(1)}, f32[127,128]{0,1:T(8,128)S(1)}, u32[]{:S(2)}, u32[]{:S(2)}) collective-permute-start(f32[127,128]{0,1:T(8,128)S(1)} %slice_bitcast_fusion.1), channel_id=1, source_target_pairs={{0,32},{32,64},{64,96},{96,128},{128,160},{160,192},{192,224},{1,3... | collective-permute-start | bytes 195080 | tf_op jit(solution)/shard_map/ppermute | solution.py:10
Sparse Core Ops, SparseCore 0:
  9.1 134.4 all-gather.5
  145.4 132.9 all-gather.7
  280.9 109.5 all-gather.9
  392.2 54.3 all-gather.11
  448.2 53.5 all-gather.13
  525.8 220.7 reduce-scatter.1
where the time goes:
time: 756 us; the launch traced here: 755 us
  waiting for transfers between devices  681 us (90%)
  matrix products  32.5 us (4%)
  other arithmetic  14.8 us (2%)
  between operations  13.6 us (2%)
    reduce_scatter x1, waiting for transfers between devices, shards(): lax.psum_scatter(partial_terms, 'chan', scatter_dimension=1, tiled=True)  221 us
    all_gather x1, waiting for transfers between devices, shards(): lax.all_gather(in_task, 'ctx', axis=0, tiled=True)  135 us
    all_gather x1, waiting for transfers between devices, shards(): lax.all_gather(in_base, 'ctx', axis=0, tiled=True)  128 us
    all_gather x1, waiting for transfers between devices, shards(): lax.all_gather(tokens, 'chan', axis=1, tiled=True)  102 us
    all_gather x1, waiting for transfers between devices, shards(): lax.all_gather(out_task, 'ctx', axis=1, tiled=True)  55.2 us
    all_gather x1, waiting for transfers between devices, shards(): lax.all_gather(out_base, 'ctx', axis=1, tiled=True)  32.5 us
    dot_general x1, matrix products, shards(): jnp.dot(gated_out, out_weight, preferred_element_type=jnp.float32)  23.9 us
  transfers between devices with their start and end apart: 8, of which 7 were waited for; matrix products, arithmetic and copies ran while one was open for 3% of the time, Pallas kernels for 0%

commit v1 on v0

v1 whole, which is shorter than its diff:
```python
import functools

import jax
import jax.numpy as jnp
from jax import lax
from jax.experimental import pallas as pl
from jax.experimental.pallas import tpu as pltpu
from jax.sharding import PartitionSpec as P

MESH = pl.DeviceIdType.MESH
NX, NZ = 4, 8
NCTX = 2 * NX
NQ = 2 * NZ
HALO = 144
bf16, f32 = jnp.bfloat16, jnp.float32


def kernel(
    rows, width, chans, short, longt,
    tok_ref, w_ref, wo_ref, feat_ref, taps_ref, decay_ref, skip_ref,
    out_ref,
    tok_all, w_all, wo_all, acc, part_in, halo_out, halo_in, proj, gate, shifts, query, filt,
    gated, msg_out, msg_in, y_out, y_in, total,
    send_sems, recv_sems, local_sems,
):
    ctx, chan = lax.axis_index("ctx"), lax.axis_index("chan")
    x, yl = ctx // 2, ctx % 2
    q, core = chan // 2, chan % 2
    yh, z = q // NZ, q % NZ
    c3 = 3 * chans

    def x_at(d):
        return ((x + d + NX) % NX) * 2 + yl, chan

    def z_at(d):
        return ctx, (yh * NZ + (z + d + NZ) % NZ) * 2 + core

    y_pair = (x * 2 + 1 - yl, chan)
    y_far = (ctx, ((1 - yh) * NZ + z) * 2 + core)
    twin = (ctx, 2 * q + 1 - core)
    after, before = ((ctx + 1) % NCTX, chan), ((ctx + NCTX - 1) % NCTX, chan)

    barrier = pltpu.get_barrier_semaphore()
    greeted = [twin, y_pair, y_far, x_at(1), x_at(-1), z_at(1), z_at(-1), after, before]
    for device in greeted:
        pl.semaphore_signal(barrier, inc=1, device_id=device, device_id_type=MESH)
    pl.semaphore_wait(barrier, len(greeted))

    copies = {}

    def send(name, src, dst, device):
        k = len(copies)
        copy = pltpu.make_async_remote_copy(
            src_ref=src, dst_ref=dst, send_sem=send_sems.at[k], recv_sem=recv_sems.at[k],
            device_id=device, device_id_type=MESH,
        )
        copy.start()
        copies[name] = copy

    def arrived(name):
        copies[name].wait_recv()

    def w_at(i, h):
        return w_all.at[pl.ds(2 * i, 2), :, pl.ds(h * c3, c3)]

    def wo_at(i, h):
        return wo_all.at[pl.ds(2 * i, 2), pl.ds(h * chans, chans), :]

    def ctx_of(d, other):
        return ((x + d + NX) % NX) * 2 + (1 - yl if other else yl)

    def tok_at(d, other):
        return tok_all.at[(1 - yh if other else yh) * NZ + (z + d + NZ) % NZ]

    send("twin_w", w_ref.at[:, 1 - core], w_at(ctx, 1), twin)
    for d in (1, -1):
        send(("tok", 0, d, 1), tok_ref, tok_at(0, 0), z_at(d))
    send("tok_y", tok_ref, tok_at(0, 0), y_far)
    for d in (1, -1):
        send(("w", 0, 0, d), w_ref.at[:, core], w_at(ctx, 0), x_at(d))
    send(("wy", 0), w_ref.at[:, core], w_at(ctx, 0), y_pair)
    send("twin_wo", wo_ref.at[:, 1 - core], wo_at(ctx, 1), twin)
    local = [
        pltpu.make_async_copy(w_ref.at[:, core], w_at(ctx, 0), local_sems.at[0]),
        pltpu.make_async_copy(wo_ref.at[:, core], wo_at(ctx, 0), local_sems.at[1]),
        pltpu.make_async_copy(tok_ref, tok_at(0, 0), local_sems.at[2]),
    ]
    for copy in local:
        copy.start()

    arrived("twin_w")
    for d in (1, -1):
        send(("w", 0, 1, d), w_at(ctx, 1), w_at(ctx, 1), x_at(d))
    send(("wy", 1), w_at(ctx, 1), w_at(ctx, 1), y_pair)
    for copy in local:
        copy.wait()
    arrived("twin_wo")
    for h in (0, 1):
        send(("woy", 0, h), wo_at(ctx, h), wo_at(ctx, h), y_pair)

    lags = lax.broadcasted_iota(jnp.int32, (longt, chans), 0).astype(f32)
    filt[...] = taps_ref[...] * jnp.exp(-decay_ref[...] * lags)
    acc[...] = jnp.zeros_like(acc)

    half = rows // 2

    def tok_step(o, step):
        for d in (1, -1):
            if step == 1:
                if not o:
                    continue
                src = tok_at(0, 1)
            else:
                arrived(("tok", o, d, step - 1))
                src = tok_at(-d * (step - 1), o)
            if step == NZ // 2:
                src = src.at[pl.ds(0 if d == 1 else half, half)]
            send(("tok", o, d, step), src, src, z_at(d))

    def w_pass(o):
        for d, h in ((1, 0), (-1, 1)):
            arrived(("w", o, h, d))
            src = w_at(ctx_of(-d, o), h)
            send(("w_far", o, d), src, src, x_at(d))

    def w_second(h):
        arrived(("wy", h))
        for d in (1, -1):
            src = w_at(ctx_of(0, 1), h)
            send(("w", 1, h, d), src, src, x_at(d))

    arrived("tok_y")
    tok_step(1, 1)
    tok_step(0, 2)
    w_second(0)
    tok_step(1, 2)
    tok_step(0, 3)
    w_second(1)
    w_pass(0)
    tok_step(1, 3)
    tok_step(0, 4)
    tok_step(1, 4)
    w_pass(1)
    for h in (0, 1):
        for d in (1, -1):
            send(("wo", h, d), wo_at(ctx, h), wo_at(ctx, h), x_at(d))
    for o in (0, 1):
        for d in (1, -1):
            arrived(("tok", o, d, NZ // 2))
            arrived(("w", o, 1 if d == 1 else 0, d))

    def accumulate(k, first, size):
        i = ((x + k // 2 + NX - 1) % NX) * 2 + k % 2
        cols = pl.ds(first, size)
        for r in range(2):
            band = pl.ds(r * half, half)
            acc[band, cols] += jnp.dot(
                tok_all[2 * i, band, :], w_all[2 * i, :, cols], preferred_element_type=f32
            ) + jnp.dot(
                tok_all[2 * i + 1, band, :], w_all[2 * i + 1, :, cols], preferred_element_type=f32
            )

    @pl.loop(0, 2 * NX - 2)
    def _(k):
        accumulate(k, 0, 2 * c3)

    for o in (0, 1):
        for d in (1, -1):
            arrived(("w_far", o, d))

    @pl.loop(2 * NX - 2, 2 * NX)
    def _(k):
        accumulate(k, c3, c3)

    send("part", acc.at[:, pl.ds(c3, c3)], part_in, twin)

    @pl.loop(2 * NX - 2, 2 * NX)
    def _(k):
        accumulate(k, 0, c3)

    for d in (1, -1):
        for h in (0, 1):
            arrived(("wo", h, d))
            src = wo_at(ctx_of(-d, 0), h)
            send(("woy", d, h), src, src, y_pair)
        src = wo_at(ctx_of(-d, 0), 0 if d == 1 else 1)
        send(("wo_far", d), src, src, x_at(d))

    arrived("part")
    last = pl.ds(rows - HALO, HALO)
    tail = (acc[last, pl.ds(0, c3)] + part_in[last, :]).astype(bf16)
    halo_out[...] = tail
    proj[pl.ds(rows, HALO), :] = tail.astype(f32)
    step_rows = (rows - HALO) // 2

    @pl.loop(0, 2)
    def _(k):
        at = pl.multiple_of(k * step_rows, 8)
        mine = (acc[pl.ds(at, step_rows), pl.ds(0, c3)] + part_in[pl.ds(at, step_rows), :]).astype(bf16)
        proj[pl.ds(pl.multiple_of(at + HALO, 8), step_rows), :] = mine.astype(f32)

    send("halo", halo_out, halo_in, after)

    def featurize(begin, count, with_query):
        size = 32

        @pl.loop(0, count // size)
        def _(k):
            at = pl.multiple_of(begin + k * size, 8)
            values = []
            for s in range(3):
                if s == 0 and not with_query:
                    values.append(None)
                    continue
                lanes = pl.ds(s * chans, chans)
                block = proj[pl.ds(pl.multiple_of(at - 8, 8), size + 8), lanes]
                value = feat_ref[0:1, lanes] * block[8:]
                for i in range(1, short):
                    value += feat_ref[i : i + 1, lanes] * block[8 - i : 8 - i + size]
                values.append(value)
            gate[pl.ds(at, size), :] = values[1] * values[2]
            if with_query:
                query[pl.ds(pl.multiple_of(at - HALO, 8), size), :] = values[0]

    def shift(begin, count):
        size = 32

        @pl.loop(0, count // size)
        def _(k):
            at = pl.multiple_of(begin + k * size, 8)
            block = gate[pl.ds(pl.multiple_of(at - 8, 8), size + 8), :]
            for r in range(8):
                shifts[r, pl.ds(at, size), :] = block[8 - r : 8 - r + size]

    tile = 64

    def convolve(begin, count):
        @pl.loop(begin, begin + count)
        def _(k):
            at = pl.multiple_of(k * tile, tile)
            own = shifts[0, pl.ds(pl.multiple_of(at + HALO, 8), tile), :]
            value = skip_ref[...] * own
            for j in range(longt):
                back, r = j - j % 8, j % 8
                value += filt[j : j + 1, :] * shifts[r, pl.ds(pl.multiple_of(at + HALO - back, 8), tile), :]
            gated[pl.ds(at, tile), pl.ds(0, chans)] = (query[pl.ds(at, tile), :] * value).astype(bf16)

    tiles = rows // tile
    first_free = 3
    featurize(HALO + 32, rows - 32, True)
    shift(HALO + 48, rows - 64)
    shift(HALO + rows - 32, 32)
    convolve(first_free, tiles - first_free)
    band = pl.ds(first_free * tile, rows - first_free * tile)
    send("gated_hi", gated.at[band, pl.ds(0, chans)], gated.at[band, pl.ds(chans, chans)], twin)

    for d in (1, -1):
        arrived(("wo_far", d))
        src = wo_at(ctx_of(2, 0), 0 if d == 1 else 1)
        send(("woy_far", d), src, src, y_pair)

    arrived("halo")
    proj[pl.ds(0, HALO), :] = jnp.where(ctx == 0, 0.0, halo_in[...].astype(f32))
    featurize(16, HALO - 16, False)
    featurize(HALO, 32, True)
    shift(24, HALO + 48)
    convolve(0, first_free)
    band = pl.ds(0, first_free * tile)
    send("gated_lo", gated.at[band, pl.ds(0, chans)], gated.at[band, pl.ds(chans, chans)], twin)
    for d in (1, -1):
        for h in (0, 1):
            arrived(("woy", d, h))
        arrived(("woy_far", d))
    for h in (0, 1):
        arrived(("woy", 0, h))
    arrived("gated_hi")
    arrived("gated_lo")

    piece = 128

    def partial(at, d, other):
        to = (1 - yh if other else yh) * NZ + (z + d + NZ) % NZ
        return jnp.dot(gated[pl.ds(at, piece), :], wo_all[to], preferred_element_type=f32)

    def message(s, j, other):
        d = 1 if s == 0 else -1
        lo = half // piece if j == 0 and d == -1 else 0
        hi = half // piece if j == 0 and d == 1 else rows // piece
        if j > 0:
            arrived(("sum", s, j - 1, other))

        def fill(begin, end, adds):
            @pl.loop(begin, end)
            def _(k):
                at = pl.multiple_of(k * piece, piece)
                value = partial(at, d * (NZ // 2 - j), other)
                if adds:
                    value += msg_in[s, j - 1, other, pl.ds(at, piece), :].astype(f32)
                msg_out[s, j, other, pl.ds(at, piece), :] = value.astype(bf16)

        if j == 1:
            mid = half // piece
            fill(0, mid, d == 1)
            fill(mid, rows // piece, d == -1)
        else:
            fill(lo, hi, j > 0)
        band = pl.ds(lo * piece, (hi - lo) * piece)
        send(("sum", s, j, other), msg_out.at[s, j, other, band], msg_in.at[s, j, other, band], z_at(d))

    for j in range(NZ // 2):
        for other in (1, 0):
            for s in (0, 1):
                message(s, j, other)

    def finish(other):
        for s in (0, 1):
            arrived(("sum", s, NZ // 2 - 1, other))

        @pl.loop(0, rows // piece)
        def _(k):
            at = pl.multiple_of(k * piece, piece)
            value = partial(at, 0, other)
            for s in (0, 1):
                value += msg_in[s, NZ // 2 - 1, other, pl.ds(at, piece), :].astype(f32)
            if other:
                y_out[pl.ds(at, piece), :] = value.astype(bf16)
            else:
                total[pl.ds(at, piece), :] = value

    finish(1)
    send("sum_y", y_out, y_in, y_far)
    finish(0)
    arrived("sum_y")
    out_ref[...] = (total[...] + y_in[...].astype(f32)).astype(bf16)
    for copy in copies.values():
        copy.wait_send()


def shards(
    tokens, in_base, in_task, feat_weight, filter_taps, decay_rates, skip_gain, out_base, out_task
):
    rows, width = tokens.shape
    chans = in_base.shape[2]
    c3 = 3 * chans
    short, longt = feat_weight.shape[0], filter_taps.shape[0]
    in_weight = (in_base.astype(f32) - in_task.astype(f32)).astype(bf16)
    in_weight = in_weight.reshape(2, 2, width, c3)
    out_weight = (out_base.astype(f32) - out_task.astype(f32)).astype(bf16)
    out_weight = out_weight.reshape(chans, 2, 2, width).transpose(1, 2, 0, 3)
    steps = NZ // 2
    vm = pltpu.VMEM
    count = 96
    return pl.pallas_call(
        functools.partial(kernel, rows, width, chans, short, longt),
        out_shape=jax.ShapeDtypeStruct((rows, width), bf16),
        in_specs=[pl.BlockSpec(memory_space=vm)] * 7,
        out_specs=pl.BlockSpec(memory_space=vm),
        scratch_shapes=[
            vm((NQ, rows, width), bf16),
            vm((NQ, width, 2 * c3), bf16),
            vm((NQ, 2 * chans, width), bf16),
            vm((rows, 2 * c3), f32),
            vm((rows, c3), f32),
            vm((HALO, c3), bf16),
            vm((HALO, c3), bf16),
            vm((HALO + rows, c3), f32),
            vm((HALO + rows, chans), f32),
            vm((8, HALO + rows, chans), f32),
            vm((rows, chans), f32),
            vm((longt, chans), f32),
            vm((rows, 2 * chans), bf16),
            vm((2, steps, 2, rows, width), bf16),
            vm((2, steps, 2, rows, width), bf16),
            vm((rows, width), bf16),
            vm((rows, width), bf16),
            vm((rows, width), f32),
            pltpu.SemaphoreType.DMA((count,)),
            pltpu.SemaphoreType.DMA((count,)),
            pltpu.SemaphoreType.DMA((3,)),
        ],
        compiler_params=pltpu.CompilerParams(
            collective_id=0, has_side_effects=True, vmem_limit_bytes=60 * 1024 * 1024
        ),
    )(
        tokens, in_weight, out_weight, feat_weight.reshape(short, c3), filter_taps,
        decay_rates.reshape(1, chans), skip_gain.reshape(1, chans),
    )


def solution(mesh):
    in_specs = (
        P("ctx", "chan"),
        P("ctx", None, "chan"),
        P("ctx", None, "chan"),
        P(None, None, "chan"),
        P(None, "chan"),
        P("chan"),
        P("chan"),
        P("chan", "ctx"),
        P("chan", "ctx"),
    )
    out_specs = P("ctx", "chan")
    return jax.shard_map(shards, mesh=mesh, in_specs=in_specs, out_specs=out_specs, check_vma=False)
```

time: 756 us -> 140 us (0.19)
  waiting for transfers between devices: 681 us -> 0 us
  Pallas kernels: 0 us -> 132 us
  matrix products: 32.5 us -> 0 us
  between operations: 13.6 us -> 0.06 us
  other arithmetic: 14.8 us -> 1.65 us
    all_gather x5 -> x0, waiting for transfers between devices: 452 us -> none  [the longest x1 135 us: shards(): lax.all_gather(in_task, 'ctx', axis=0, tiled=True)]
    reduce_scatter x1 -> x0, waiting for transfers between devices: 221 us -> none  [shards(): lax.psum_scatter(partial_terms, 'chan', scatter_dimension=1, tiled=True)]
    pallas_call x0 -> x1, Pallas kernels: none -> 132 us  [shards(): pl.pallas_call(functools.partial(kernel, rows, width, chans, short, longt...]
    dot_general x2 -> x0, matrix products: 32.5 us -> none  [the longest x1 23.9 us: shards(): jnp.dot(gated_out, out_weight, preferred_element_type=jnp.float32)]
    convert_element_type x2, other arithmetic: 11.7 us -> 1.65 us  [the longest x1 1.57 us: shards(): in_weight = (in_base.astype(f32) - in_task.astype(f32)).astype(bf16)]
  transfers between devices with their start and end apart: 8 -> 0, of which waited for: 7 -> 0; matrix products, arithmetic and copies ran while one was open for 3% -> 0% of each run, Pallas kernels for 0% -> 0%
where the time goes in v1:
time: 140 us; the launch traced here: 138 us
  Pallas kernels  132 us (94%)
  local copies, waits for them, and re-layouts  4.98 us (4%)
  other arithmetic  1.65 us (1%)
    pallas_call x1, Pallas kernels, shards(): pl.pallas_call(functools.partial(kernel, rows, width, chans, short, longt...  132 us

profile of v1, /device:TPU:4, one launch (start us, length us, event | category | flops | bytes accessed | tf_op | source)
XLA Modules:
  0.0 138.3 jit_solution(1075946079850410889)
XLA Ops:
  0.0 1.6 %subtract_convert_fusion = bf16[1024,3,128]{2,0,1:T(8,128)(2,1)S(1)} fusion(bf16[1024,3,128]{2,0,1:T(8,128)(2,1)} %param.11, bf16[1024,3,128]{2,0,1:T(8,128)(2,1)} %param.10), kind=kLoop, calls=%fused_computation | loop fusion | flops 1572864 | bytes 2359296 | tf_op jit(solution)/shard_map/convert_element_type | solution.py:346
  1.6 0.7 copy.16
  2.3 0.0 copy-start
  2.3 0.0 copy-start.1
  2.3 1.4 %reshape.20.w_ref = bf16[2,2,256,384]{3,2,1,0:T(8,128)(2,1)} reshape(bf16[1024,3,128]{2,1,0:T(4,128)(2,1)S(1)} %copy.16) | data formatting | bytes 1572864 | tf_op jit(solution)/shard_map/reshape | solution.py:347
  3.7 0.0 copy-done
  3.7 0.2 copy.12
  3.9 0.0 copy-done.1
  3.9 0.2 copy.13
  4.1 0.1 subtract_convert_fusion.1
  4.2 0.9 copy.14
  5.0 131.6 %shard_map.91 = bf16[512,256]{1,0:T(8,128)(2,1)} custom-call(bf16[512,256]{1,0:T(8,128)(2,1)} %tok_ref.1, bf16[2,2,256,384]{3,2,1,0:T(8,128)(2,1)} %reshape.20.w_ref, bf16[2,2,128,256]{3,2,1,0:T(8,128)(2,1)} %bitcast.6, f32[7,384]{1,0:T(8,128)} %bitcast.7, f32[128,128]{1,0:T(8,128)} %taps_ref.1, f32[1,128]{1,0:T(1,128)} %bitcast.8, f32[1,128]{1,0:T(1,128)} %bitcast.9), custom_call_target="tpu_custom_call" | custom-call | tf_op jit(solution)/shard_map/pallas_call | solution.py:353
  136.6 1.7 %copy.19 = bf16[512,256]{1,0:T(8,128)(2,1)} copy(bf16[512,256]{1,0:T(8,128)(2,1)} %shard_map.91) | data formatting | bytes 524288
Async XLA Ops:
  2.3 1.5 %copy-start = (bf16[128,1024]{1,0:T(8,128)(2,1)S(1)}, bf16[128,1024]{1,0:T(8,128)(2,1)}, u32[]{:S(2)}) copy-start(bf16[128,1024]{1,0:T(8,128)(2,1)} %param.16) | copy-start | bytes 786436
  2.3 1.6 %copy-start.1 = (bf16[128,1024]{1,0:T(8,128)(2,1)S(1)}, bf16[128,1024]{1,0:T(8,128)(2,1)}, u32[]{:S(2)}) copy-start(bf16[128,1024]{1,0:T(8,128)(2,1)} %param.17) | copy-start | bytes 786436

commit v2 on v1

--- a/solution.py
+++ b/solution.py
@@ -17,10 +17,10 @@
 
 def kernel(
     rows, width, chans, short, longt,
-    tok_ref, w_ref, wo_ref, feat_ref, taps_ref, decay_ref, skip_ref,
-    out_ref,
-    tok_all, w_all, wo_all, acc, part_in, halo_out, halo_in, proj, gate, shifts, query, filt,
-    gated, msg_out, msg_in, y_out, y_in, total,
+    tok_ref, base_ref, task_ref, obase_ref, otask_ref, feat_ref, taps_ref, decay_ref, skip_ref,
+    total, y_in,
+    base, task, obase, otask, w_twin, wo_twin, tok_all, w_all, wo_all, acc, part_in, halo_out, halo_in, proj, gate, shifts, query, filt,
+    gated, msg_out, msg_in, y_out,
     send_sems, recv_sems, local_sems,
 ):
     ctx, chan = lax.axis_index("ctx"), lax.axis_index("chan")
@@ -39,6 +39,15 @@
     y_far = (ctx, ((1 - yh) * NZ + z) * 2 + core)
     twin = (ctx, 2 * q + 1 - core)
     after, before = ((ctx + 1) % NCTX, chan), ((ctx + NCTX - 1) % NCTX, chan)
+
+    local = [
+        pltpu.make_async_copy(src, dst, local_sems.at[k])
+        for k, (src, dst) in enumerate(
+            [(base_ref, base), (task_ref, task), (obase_ref, obase), (otask_ref, otask), (tok_ref, tok_all.at[q])]
+        )
+    ]
+    for copy in local:
+        copy.start()
 
     barrier = pltpu.get_barrier_semaphore()
     greeted = [twin, y_pair, y_far, x_at(1), x_at(-1), z_at(1), z_at(-1), after, before]
@@ -61,7 +70,7 @@
         copies[name].wait_recv()
 
     def w_at(i, h):
-        return w_all.at[pl.ds(2 * i, 2), :, pl.ds(h * c3, c3)]
+        return w_all.at[pl.ds(2 * i, 2), h]
 
     def wo_at(i, h):
         return wo_all.at[pl.ds(2 * i, 2), pl.ds(h * chans, chans), :]
@@ -72,28 +81,49 @@
     def tok_at(d, other):
         return tok_all.at[(1 - yh if other else yh) * NZ + (z + d + NZ) % NZ]
 
-    send("twin_w", w_ref.at[:, 1 - core], w_at(ctx, 1), twin)
     for d in (1, -1):
         send(("tok", 0, d, 1), tok_ref, tok_at(0, 0), z_at(d))
     send("tok_y", tok_ref, tok_at(0, 0), y_far)
-    for d in (1, -1):
-        send(("w", 0, 0, d), w_ref.at[:, core], w_at(ctx, 0), x_at(d))
-    send(("wy", 0), w_ref.at[:, core], w_at(ctx, 0), y_pair)
-    send("twin_wo", wo_ref.at[:, 1 - core], wo_at(ctx, 1), twin)
-    local = [
-        pltpu.make_async_copy(w_ref.at[:, core], w_at(ctx, 0), local_sems.at[0]),
-        pltpu.make_async_copy(wo_ref.at[:, core], wo_at(ctx, 0), local_sems.at[1]),
-        pltpu.make_async_copy(tok_ref, tok_at(0, 0), local_sems.at[2]),
-    ]
-    for copy in local:
-        copy.start()
+
+    def less(one, two):
+        return (one.astype(f32) - two.astype(f32)).astype(bf16)
+
+    local[0].wait()
+    local[1].wait()
+    for owner in (1 - core, core):
+        is_twin = owner is not core
+        for b in range(2):
+            @pl.loop(0, 3)
+            def _(s):
+                band = pl.ds(pl.multiple_of((2 * b + owner) * width, width), width)
+                value = less(base[s, band, :], task[s, band, :])
+                if is_twin:
+                    w_twin[b, s] = value
+                else:
+                    w_all[2 * ctx + b, 0, s] = value
+
+    send("twin_w", w_twin, w_at(ctx, 1), twin)
+    for d in (1, -1):
+        send(("w", 0, 0, d), w_at(ctx, 0), w_at(ctx, 0), x_at(d))
+    send(("wy", 0), w_at(ctx, 0), w_at(ctx, 0), y_pair)
+    local[2].wait()
+    local[3].wait()
+    for owner in (1 - core, core):
+        is_twin = owner is not core
+        for b in range(2):
+            band = pl.ds(pl.multiple_of((2 * b + owner) * width, width), width)
+            value = less(obase[:, band], otask[:, band])
+            if is_twin:
+                wo_twin[b] = value
+            else:
+                wo_all[2 * ctx + b, pl.ds(0, chans), :] = value
+    send("twin_wo", wo_twin, wo_at(ctx, 1), twin)
 
     arrived("twin_w")
     for d in (1, -1):
         send(("w", 0, 1, d), w_at(ctx, 1), w_at(ctx, 1), x_at(d))
     send(("wy", 1), w_at(ctx, 1), w_at(ctx, 1), y_pair)
-    for copy in local:
-        copy.wait()
+    local[4].wait()
     arrived("twin_wo")
     for h in (0, 1):
         send(("woy", 0, h), wo_at(ctx, h), wo_at(ctx, h), y_pair)
@@ -152,12 +182,17 @@
     def accumulate(k, first, size):
         i = ((x + k // 2 + NX - 1) % NX) * 2 + k % 2
         cols = pl.ds(first, size)
+
+        def weights(k):
+            parts = [divmod(t, 3) for t in range(first // chans, (first + size) // chans)]
+            return jnp.concatenate([w_all[k, h, s] for h, s in parts], axis=1)
+
         for r in range(2):
             band = pl.ds(r * half, half)
             acc[band, cols] += jnp.dot(
-                tok_all[2 * i, band, :], w_all[2 * i, :, cols], preferred_element_type=f32
+                tok_all[2 * i, band, :], weights(2 * i), preferred_element_type=f32
             ) + jnp.dot(
-                tok_all[2 * i + 1, band, :], w_all[2 * i + 1, :, cols], preferred_element_type=f32
+                tok_all[2 * i + 1, band, :], weights(2 * i + 1), preferred_element_type=f32
             )
 
     @pl.loop(0, 2 * NX - 2)
@@ -331,7 +366,6 @@
     send("sum_y", y_out, y_in, y_far)
     finish(0)
     arrived("sum_y")
-    out_ref[...] = (total[...] + y_in[...].astype(f32)).astype(bf16)
     for copy in copies.values():
         copy.wait_send()
 
@@ -343,21 +377,23 @@
     chans = in_base.shape[2]
     c3 = 3 * chans
     short, longt = feat_weight.shape[0], filter_taps.shape[0]
-    in_weight = (in_base.astype(f32) - in_task.astype(f32)).astype(bf16)
-    in_weight = in_weight.reshape(2, 2, width, c3)
-    out_weight = (out_base.astype(f32) - out_task.astype(f32)).astype(bf16)
-    out_weight = out_weight.reshape(chans, 2, 2, width).transpose(1, 2, 0, 3)
     steps = NZ // 2
-    vm = pltpu.VMEM
-    count = 96
-    return pl.pallas_call(
+    vm, count = pltpu.VMEM, 96
+    in_vmem, anywhere = pl.BlockSpec(memory_space=vm), pl.BlockSpec(memory_space=pl.ANY)
+    total, across = pl.pallas_call(
         functools.partial(kernel, rows, width, chans, short, longt),
-        out_shape=jax.ShapeDtypeStruct((rows, width), bf16),
-        in_specs=[pl.BlockSpec(memory_space=vm)] * 7,
-        out_specs=pl.BlockSpec(memory_space=vm),
+        out_shape=[jax.ShapeDtypeStruct((rows, width), f32), jax.ShapeDtypeStruct((rows, width), bf16)],
+        in_specs=[anywhere] * 5 + [in_vmem] * 4,
+        out_specs=[in_vmem] * 2,
         scratch_shapes=[
+            vm((3, in_base.shape[0], chans), bf16),
+            vm((3, in_base.shape[0], chans), bf16),
+            vm(out_base.shape, bf16),
+            vm(out_base.shape, bf16),
+            vm((2, 3, width, chans), bf16),
+            vm((2, chans, width), bf16),
             vm((NQ, rows, width), bf16),
-            vm((NQ, width, 2 * c3), bf16),
+            vm((NQ, 2, 3, width, chans), bf16),
             vm((NQ, 2 * chans, width), bf16),
             vm((rows, 2 * c3), f32),
             vm((rows, c3), f32),
@@ -372,19 +408,18 @@
             vm((2, steps, 2, rows, width), bf16),
             vm((2, steps, 2, rows, width), bf16),
             vm((rows, width), bf16),
-            vm((rows, width), bf16),
-            vm((rows, width), f32),
             pltpu.SemaphoreType.DMA((count,)),
             pltpu.SemaphoreType.DMA((count,)),
-            pltpu.SemaphoreType.DMA((3,)),
+            pltpu.SemaphoreType.DMA((5,)),
         ],
         compiler_params=pltpu.CompilerParams(
             collective_id=0, has_side_effects=True, vmem_limit_bytes=60 * 1024 * 1024
         ),
     )(
-        tokens, in_weight, out_weight, feat_weight.reshape(short, c3), filter_taps,
-        decay_rates.reshape(1, chans), skip_gain.reshape(1, chans),
+        tokens, in_base.transpose(1, 0, 2), in_task.transpose(1, 0, 2), out_base, out_task,
+        feat_weight.reshape(short, c3), filter_taps, decay_rates.reshape(1, chans), skip_gain.reshape(1, chans),
     )
+    return (total + across.astype(f32)).astype(bf16)
 
 
 def solution(mesh):

time: 140 us -> 135 us (0.964)
  local copies, waits for them, and re-layouts: 4.98 us -> 0 us
    reshape x3 -> x0, local copies, waits for them, and re-layouts: 2.96 us -> none  [the longest x2 2.11 us: shards(): in_weight = in_weight.reshape(2, 2, width, c3)]
    unnamed x7 -> x0, local copies, waits for them, and re-layouts: 2.02 us -> none
where the time goes in v2:
time: 135 us; the launch traced here: 133 us
  Pallas kernels  132 us (98%)
  other arithmetic  1.87 us (1%)
    pallas_call x1, Pallas kernels, shards(): pl.pallas_call(functools.partial(kernel, rows, width, chans, short, longt...  132 us

profile of v2, /device:TPU:4, one launch (start us, length us, event | category | flops | bytes accessed | tf_op | source)
XLA Modules:
  0.0 133.4 jit_solution(15797887794936044976)
XLA Ops:
  0.0 131.5 %shard_map.91 = (f32[512,256]{1,0:T(8,128)}, bf16[512,256]{1,0:T(8,128)(2,1)}) custom-call(bf16[512,256]{1,0:T(8,128)(2,1)} %tok_ref.1, bf16[3,1024,128]{2,1,0:T(8,128)(2,1)} %bitcast.5, bf16[3,1024,128]{2,1,0:T(8,128)(2,1)} %bitcast.6, bf16[128,1024]{1,0:T(8,128)(2,1)} %obase_ref.1, bf16[128,1024]{1,0:T(8,128)(2,1)} %otask_ref.1, f32[7,384]{1,0:T(8,128)} %bitcast.7, ...), custom_call_target="tpu_custom_call" | custom-call | tf_op jit(solution)/shard_map/pallas_call | solution.py:383
  131.5 1.9 %add_convert_fusion = bf16[512,256]{1,0:T(8,128)(2,1)} fusion(f32[512,256]{1,0:T(8,128)} %get-tuple-element.7, bf16[512,256]{1,0:T(8,128)(2,1)} %get-tuple-element.8), kind=kLoop, calls=%fused_computation | loop fusion | flops 393216 | bytes 1048576 | tf_op jit(solution)/shard_map/convert_element_type | solution.py:422

commit v3 on v2

--- a/solution.py
+++ b/solution.py
@@ -18,9 +18,9 @@
 def kernel(
     rows, width, chans, short, longt,
     tok_ref, base_ref, task_ref, obase_ref, otask_ref, feat_ref, taps_ref, decay_ref, skip_ref,
-    total, y_in,
+    out_ref,
     base, task, obase, otask, w_twin, wo_twin, tok_all, w_all, wo_all, acc, part_in, halo_out, halo_in, proj, gate, shifts, query, filt,
-    gated, msg_out, msg_in, y_out,
+    gated, msg_out, msg_in, first_out, first_in, y_out, y_in, total,
     send_sems, recv_sems, local_sems,
 ):
     ctx, chan = lax.axis_index("ctx"), lax.axis_index("chan")
@@ -69,8 +69,8 @@
     def arrived(name):
         copies[name].wait_recv()
 
-    def w_at(i, h):
-        return w_all.at[pl.ds(2 * i, 2), h]
+    def w_at(i, h, begin=0, end=3):
+        return w_all.at[pl.ds(2 * i, 2), h, pl.ds(begin, end - begin)]
 
     def wo_at(i, h):
         return wo_all.at[pl.ds(2 * i, 2), pl.ds(h * chans, chans), :]
@@ -125,8 +125,7 @@
     send(("wy", 1), w_at(ctx, 1), w_at(ctx, 1), y_pair)
     local[4].wait()
     arrived("twin_wo")
-    for h in (0, 1):
-        send(("woy", 0, h), wo_at(ctx, h), wo_at(ctx, h), y_pair)
+    send(("woy", 0), wo_at(ctx, 0), wo_at(ctx, 0), y_pair)
 
     lags = lax.broadcasted_iota(jnp.int32, (longt, chans), 0).astype(f32)
     filt[...] = taps_ref[...] * jnp.exp(-decay_ref[...] * lags)
@@ -147,37 +146,65 @@
                 src = src.at[pl.ds(0 if d == 1 else half, half)]
             send(("tok", o, d, step), src, src, z_at(d))
 
-    def w_pass(o):
-        for d, h in ((1, 0), (-1, 1)):
-            arrived(("w", o, h, d))
-            src = w_at(ctx_of(-d, o), h)
-            send(("w_far", o, d), src, src, x_at(d))
+    way = {1: 0, -1: 1}
+
+    def w_first(h):
+        for d in (1, -1):
+            arrived(("w", 0, h, d))
+            src = w_at(ctx_of(-d, 0), h)
+            if way[d] == h:
+                send(("w_far", 0, d), src, src, x_at(d))
+            src = w_at(ctx_of(-d, 0), h, 2, 3)
+            send(("wy", d, h), src, src, y_pair)
 
     def w_second(h):
         arrived(("wy", h))
         for d in (1, -1):
-            src = w_at(ctx_of(0, 1), h)
+            src = w_at(ctx_of(0, 1), h, 0, 2)
             send(("w", 1, h, d), src, src, x_at(d))
+
+    def w_third(h):
+        for d in (1, -1):
+            arrived(("w", 1, h, d))
+            if way[d] == h:
+                src = w_at(ctx_of(-d, 1), h, 0, 2)
+                send(("w_far", 1, d), src, src, x_at(d))
+
+    def w_last():
+        for d in (1, -1):
+            arrived(("w_far", 0, d))
+            src = w_at(ctx_of(2, 0), way[d], 2, 3)
+            send(("wy_far", d), src, src, y_pair)
 
     arrived("tok_y")
     tok_step(1, 1)
     tok_step(0, 2)
+    w_first(0)
     w_second(0)
     tok_step(1, 2)
     tok_step(0, 3)
+    w_first(1)
     w_second(1)
-    w_pass(0)
     tok_step(1, 3)
+    w_last()
+    send(("woy", 1), wo_at(ctx, 1), wo_at(ctx, 1), y_pair)
     tok_step(0, 4)
+    w_third(0)
     tok_step(1, 4)
-    w_pass(1)
+    w_third(1)
     for h in (0, 1):
         for d in (1, -1):
-            send(("wo", h, d), wo_at(ctx, h), wo_at(ctx, h), x_at(d))
+            send(("wo", 0, h, d), wo_at(ctx, h), wo_at(ctx, h), x_at(d))
+    arrived(("woy", 0))
+    for d in (1, -1):
+        src = wo_at(ctx_of(0, 1), 0)
+        send(("wo", 1, 0, d), src, src, x_at(d))
     for o in (0, 1):
         for d in (1, -1):
             arrived(("tok", o, d, NZ // 2))
-            arrived(("w", o, 1 if d == 1 else 0, d))
+    for d in (1, -1):
+        for h in (0, 1):
+            arrived(("wy", d, h))
 
     def accumulate(k, first, size):
         i = ((x + k // 2 + NX - 1) % NX) * 2 + k % 2
@@ -199,9 +226,9 @@
     def _(k):
         accumulate(k, 0, 2 * c3)
 
-    for o in (0, 1):
-        for d in (1, -1):
-            arrived(("w_far", o, d))
+    for d in (1, -1):
+        arrived(("w_far", 1, d))
+        arrived(("wy_far", d))
 
     @pl.loop(2 * NX - 2, 2 * NX)
     def _(k):
@@ -213,13 +240,24 @@
     def _(k):
         accumulate(k, 0, c3)
 
-    for d in (1, -1):
-        for h in (0, 1):
-            arrived(("wo", h, d))
-            src = wo_at(ctx_of(-d, 0), h)
-            send(("woy", d, h), src, src, y_pair)
-        src = wo_at(ctx_of(-d, 0), 0 if d == 1 else 1)
-        send(("wo_far", d), src, src, x_at(d))
+    def wo_pass():
+        for h in (1, 0):
+            for d in (1, -1):
+                arrived(("wo", 0, h, d))
+                src = wo_at(ctx_of(-d, 0), h)
+                if way[d] == h:
+                    send(("wo_far", 0, d), src, src, x_at(d))
+                if h == 1:
+                    send(("wo_y", d), src, src, y_pair)
+        for d in (1, -1):
+            arrived(("wo", 1, 0, d))
+            src = wo_all.at[2 * ctx_of(-d, 1) + way[d], pl.ds(0, chans), :]
+            send(("wo_far", 1, d), src, src, x_at(d))
+
+    def wo_last():
+        arrived(("wo_far", 0, -1))
+        src = wo_at(ctx_of(2, 0), 1)
+        send("wo_y_far", src, src, y_pair)
 
     arrived("part")
     last = pl.ds(rows - HALO, HALO)
@@ -280,92 +318,96 @@
                 value += filt[j : j + 1, :] * shifts[r, pl.ds(pl.multiple_of(at + HALO - back, 8), tile), :]
             gated[pl.ds(at, tile), pl.ds(0, chans)] = (query[pl.ds(at, tile), :] * value).astype(bf16)
 
-    tiles = rows // tile
-    first_free = 3
-    featurize(HALO + 32, rows - 32, True)
-    shift(HALO + 48, rows - 64)
-    shift(HALO + rows - 32, 32)
-    convolve(first_free, tiles - first_free)
-    band = pl.ds(first_free * tile, rows - first_free * tile)
+    tiles = half // tile
+    upper = HALO + half - 112
+    featurize(upper - 48, HALO + rows - upper + 48, True)
+    shift(upper - 16, HALO + rows - upper + 16)
+    convolve(tiles, tiles)
+    band = pl.ds(half, half)
     send("gated_hi", gated.at[band, pl.ds(0, chans)], gated.at[band, pl.ds(chans, chans)], twin)
-
-    for d in (1, -1):
-        arrived(("wo_far", d))
-        src = wo_at(ctx_of(2, 0), 0 if d == 1 else 1)
-        send(("woy_far", d), src, src, y_pair)
+    wo_pass()
 
     arrived("halo")
     proj[pl.ds(0, HALO), :] = jnp.where(ctx == 0, 0.0, halo_in[...].astype(f32))
     featurize(16, HALO - 16, False)
-    featurize(HALO, 32, True)
-    shift(24, HALO + 48)
-    convolve(0, first_free)
-    band = pl.ds(0, first_free * tile)
+    featurize(HALO, upper - 48 - HALO, True)
+    shift(24, upper - 32)
+    convolve(0, tiles)
+    band = pl.ds(0, half)
     send("gated_lo", gated.at[band, pl.ds(0, chans)], gated.at[band, pl.ds(chans, chans)], twin)
-    for d in (1, -1):
-        for h in (0, 1):
-            arrived(("woy", d, h))
-        arrived(("woy_far", d))
-    for h in (0, 1):
-        arrived(("woy", 0, h))
+    wo_last()
+    for d in (1, -1):
+        arrived(("wo_y", d))
+        arrived(("wo_far", 1, d))
+    arrived(("wo_far", 0, 1))
+    arrived(("woy", 1))
+    arrived("wo_y_far")
     arrived("gated_hi")
-    arrived("gated_lo")
-
-    piece = 128
+
+    piece = half // 2
+    order = [4, 3, -3, 2, -2, 1, -1, 0]
 
     def partial(at, d, other):
         to = (1 - yh if other else yh) * NZ + (z + d + NZ) % NZ
         return jnp.dot(gated[pl.ds(at, piece), :], wo_all[to], preferred_element_type=f32)
 
-    def message(s, j, other):
-        d = 1 if s == 0 else -1
-        lo = half // piece if j == 0 and d == -1 else 0
-        hi = half // piece if j == 0 and d == 1 else rows // piece
-        if j > 0:
-            arrived(("sum", s, j - 1, other))
-
-        def fill(begin, end, adds):
-            @pl.loop(begin, end)
-            def _(k):
-                at = pl.multiple_of(k * piece, piece)
-                value = partial(at, d * (NZ // 2 - j), other)
-                if adds:
-                    value += msg_in[s, j - 1, other, pl.ds(at, piece), :].astype(f32)
-                msg_out[s, j, other, pl.ds(at, piece), :] = value.astype(bf16)
-
-        if j == 1:
-            mid = half // piece
-            fill(0, mid, d == 1)
-            fill(mid, rows // piece, d == -1)
-        else:
-            fill(lo, hi, j > 0)
-        band = pl.ds(lo * piece, (hi - lo) * piece)
-        send(("sum", s, j, other), msg_out.at[s, j, other, band], msg_in.at[s, j, other, band], z_at(d))
-
-    for j in range(NZ // 2):
-        for other in (1, 0):
+    def part(p):
+        return pl.ds(pl.multiple_of(p * piece, piece), piece)
+
+    def base_row(kind):
+        return 0 if kind == 2 else half
+
+    def message(kind, j):
+        for s, d in enumerate((1, -1)):
+            if j > 0:
+                arrived(("sum", kind, s, j - 1))
+            slot = order.index(abs(4 - j) if j == 0 else d * (4 - j))
+            if kind == 2 and (j > 0 or s == 0):
+                arrived(("first", slot))
+            pieces = (way[d],) if j == 0 else (0, 1)
+            for p in pieces:
+                value = partial(base_row(kind) + p * piece, d * (4 - j), kind == 0)
+                if kind == 2:
+                    value += first_in[slot, part(p), :].astype(f32)
+                if j > 1 or (j == 1 and p == way[d]):
+                    value += msg_in[s, j - 1, kind, part(p), :].astype(f32)
+                msg_out[s, j, kind, part(p), :] = value.astype(bf16)
+            band = pl.ds(pieces[0] * piece, len(pieces) * piece)
+            send(("sum", kind, s, j), msg_out.at[s, j, kind, band], msg_in.at[s, j, kind, band], z_at(d))
+
+    def finish(kind):
+        for s in (0, 1):
+            arrived(("sum", kind, s, 3))
+        if kind == 2:
+            arrived(("first", order.index(0)))
+        for p in (0, 1):
+            value = partial(base_row(kind) + p * piece, 0, kind == 0)
             for s in (0, 1):
-                message(s, j, other)
-
-    def finish(other):
-        for s in (0, 1):
-            arrived(("sum", s, NZ // 2 - 1, other))
-
-        @pl.loop(0, rows // piece)
-        def _(k):
-            at = pl.multiple_of(k * piece, piece)
-            value = partial(at, 0, other)
-            for s in (0, 1):
-                value += msg_in[s, NZ // 2 - 1, other, pl.ds(at, piece), :].astype(f32)
-            if other:
-                y_out[pl.ds(at, piece), :] = value.astype(bf16)
+                value += msg_in[s, 3, kind, part(p), :].astype(f32)
+            if kind == 0:
+                y_out[part(p), :] = value.astype(bf16)
+            elif kind == 1:
+                total[part(p), :] = value
             else:
-                total[pl.ds(at, piece), :] = value
-
+                value += first_in[order.index(0), part(p), :].astype(f32)
+                out_ref[part(p), :] = value.astype(bf16)
+
+    message(0, 0)
+    message(1, 0)
+    arrived("gated_lo")
+    for slot, d in enumerate(order):
+        for p in (0, 1):
+            first_out[slot, part(p), :] = partial(p * piece, d, True).astype(bf16)
+        send(("first", slot), first_out.at[slot], first_in.at[slot], y_far)
+    for kind, j in [(0, 1), (2, 0), (1, 1), (0, 2), (2, 1), (1, 2), (0, 3), (2, 2), (1, 3)]:
+        message(kind, j)
+    finish(0)
+    send("sum_y", y_out, y_in, y_far)
+    message(2, 3)
     finish(1)
-    send("sum_y", y_out, y_in, y_far)
-    finish(0)
+    finish(2)
     arrived("sum_y")
+    out_ref[pl.ds(half, half), :] = (total[...] + y_in[...].astype(f32)).astype(bf16)
     for copy in copies.values():
         copy.wait_send()
 
@@ -377,14 +419,13 @@
     chans = in_base.shape[2]
     c3 = 3 * chans
     short, longt = feat_weight.shape[0], filter_taps.shape[0]
-    steps = NZ // 2
     vm, count = pltpu.VMEM, 96
     in_vmem, anywhere = pl.BlockSpec(memory_space=vm), pl.BlockSpec(memory_space=pl.ANY)
-    total, across = pl.pallas_call(
+    return pl.pallas_call(
         functools.partial(kernel, rows, width, chans, short, longt),
-        out_shape=[jax.ShapeDtypeStruct((rows, width), f32), jax.ShapeDtypeStruct((rows, width), bf16)],
+        out_shape=jax.ShapeDtypeStruct((rows, width), bf16),
         in_specs=[anywhere] * 5 + [in_vmem] * 4,
-        out_specs=[in_vmem] * 2,
+        out_specs=in_vmem,
         scratch_shapes=[
             vm((3, in_base.shape[0], chans), bf16),
             vm((3, in_base.shape[0], chans), bf16),
@@ -405,9 +446,13 @@
             vm((rows, chans), f32),
             vm((longt, chans), f32),
             vm((rows, 2 * chans), bf16),
-            vm((2, steps, 2, rows, width), bf16),
-            vm((2, steps, 2, rows, width), bf16),
-            vm((rows, width), bf16),
+            vm((2, NZ // 2, 3, rows // 2, width), bf16),
+            vm((2, NZ // 2, 3, rows // 2, width), bf16),
+            vm((NZ, rows // 2, width), bf16),
+            vm((NZ, rows // 2, width), bf16),
+            vm((rows // 2, width), bf16),
+            vm((rows // 2, width), bf16),
+            vm((rows // 2, width), f32),
             pltpu.SemaphoreType.DMA((count,)),
             pltpu.SemaphoreType.DMA((count,)),
             pltpu.SemaphoreType.DMA((5,)),
@@ -419,7 +464,6 @@
         tokens, in_base.transpose(1, 0, 2), in_task.transpose(1, 0, 2), out_base, out_task,
         feat_weight.reshape(short, c3), filter_taps, decay_rates.reshape(1, chans), skip_gain.reshape(1, chans),
     )
-    return (total + across.astype(f32)).astype(bf16)
 
 
 def solution(mesh):

time: 135 us -> 111 us (0.82)
  Pallas kernels: 132 us -> 108 us
  other arithmetic: 1.87 us -> 0 us
  local copies, waits for them, and re-layouts: 0 us -> 1.67 us
    pallas_call x1, Pallas kernels: 132 us -> 108 us  [shards(): pl.pallas_call(functools.partial(kernel, rows, width, chans, short, longt...]
    convert_element_type x1 -> x0, other arithmetic: 1.87 us -> none  [shards(): return (total + across.astype(f32)).astype(bf16)]
    unnamed x0 -> x1, local copies, waits for them, and re-layouts: none -> 1.67 us
where the time goes in v3:
time: 111 us; the launch traced here: 110 us
  Pallas kernels  108 us (97%)
  local copies, waits for them, and re-layouts  1.67 us (2%)
    pallas_call x1, Pallas kernels, shards(): pl.pallas_call(functools.partial(kernel, rows, width, chans, short, longt...  108 us

profile of v3, /device:TPU:4, one launch (start us, length us, event | category | flops | bytes accessed | tf_op | source)
XLA Modules:
  0.0 110.1 jit_solution(6150725505897867838)
XLA Ops:
  0.0 108.4 %shard_map.91 = bf16[512,256]{1,0:T(8,128)(2,1)} custom-call(bf16[512,256]{1,0:T(8,128)(2,1)} %tok_ref.1, bf16[3,1024,128]{2,1,0:T(8,128)(2,1)} %bitcast.5, bf16[3,1024,128]{2,1,0:T(8,128)(2,1)} %bitcast.6, bf16[128,1024]{1,0:T(8,128)(2,1)} %obase_ref.1, bf16[128,1024]{1,0:T(8,128)(2,1)} %otask_ref.1, f32[7,384]{1,0:T(8,128)} %bitcast.7, ...), custom_call_target="tpu_custom_call" | custom-call | tf_op jit(solution)/shard_map/pallas_call | solution.py:424
  108.4 1.7 %copy.11 = bf16[512,256]{1,0:T(8,128)(2,1)} copy(bf16[512,256]{1,0:T(8,128)(2,1)} %shard_map.91) | data formatting | bytes 524288
